TPU v7x, 32 devices: a whole 2x2x4 slice. The times are simulated.
32 devices in a mesh: bank: 8 (over z, y), grp: 4 (over x, core).
Axes of the slice: x: 2, y: 2, z: 4, core: 2. Of those that a mesh axis runs over, the one named last changes fastest.
Arguments:
- users: bfloat16 [4096, 256], P(('bank', 'grp')), may hold values from -32 to 32
- bank: bfloat16 [4096, 256], P('bank'), may hold values from -3 to 3
- positives: int32 [4096], P(('bank', 'grp')), may hold values from 0 to 4095
- cohorts: int32 [4096], P(('bank', 'grp')), may hold values from 0 to 15
Outputs:
- loss: float32 [], replicated
- user_grad: float32 [4096, 256], P(('bank', 'grp'))
- bank_grad: float32 [4096, 256], P(('bank', 'grp'))
All inputs are finite; a program needn't handle non-finite values.
Results may differ from a plain program's by a relative error of at most 0.014.
Values may be sent and summed in bfloat16 or wider, within the bound.
A program may use at most 64 MiB of HBM per device.

v0:
```python
import jax
import jax.numpy as jnp
from jax import lax
from jax.sharding import PartitionSpec as P

NCOH = 16


def make_dlogits(upart, local_pos, weight, lse, bank):
    logits = jnp.dot(upart, bank.T, preferred_element_type=jnp.float32)
    item_ids = jnp.arange(bank.shape[0], dtype=jnp.int32)
    hot = (item_ids[None, :] == local_pos[:, None]).astype(jnp.float32)
    prob = jnp.exp(logits - lse[:, None])
    return (weight[:, None] * (prob - hot)).astype(jnp.bfloat16)


def per_device(users, bank, positives, cohorts):
    per_dev = users.shape[0]
    items_here = bank.shape[0]
    bank_size = lax.axis_size("bank")
    total_users = per_dev * bank_size * lax.axis_size("grp")
    cohort_ids = jnp.arange(NCOH, dtype=jnp.int32)
    local_counts = jnp.sum((cohorts[:, None] == cohort_ids[None, :]).astype(jnp.float32), axis=0)
    counts = lax.psum(local_counts, ("bank", "grp"))
    gathered, gpos, gcoh = (
        lax.all_gather(users, "bank", axis=0, tiled=True),
        lax.all_gather(positives, "bank", axis=0, tiled=True),
        lax.all_gather(cohorts, "bank", axis=0, tiled=True),
    )
    rows = gathered.shape[0]
    own = jnp.sum(
        jnp.where(gcoh[:, None] == cohort_ids[None, :], counts[None, :], jnp.float32(0.0)), axis=1
    )
    weight = jnp.float32(total_users) / NCOH / own
    local_pos = gpos - lax.axis_index("bank") * items_here
    block = 512
    count = rows // block
    ublocks = gathered.reshape(count, block, gathered.shape[1])
    pblocks = local_pos.reshape(count, block)
    item_ids = jnp.arange(items_here, dtype=jnp.int32)

    def forward(carry, parts):
        upart, ppart = parts
        logits = jnp.dot(upart, bank.T, preferred_element_type=jnp.float32)
        top = jnp.max(logits, axis=1)
        total = jnp.sum(jnp.exp(logits - top[:, None]), axis=1)
        pos_logit = jnp.sum(
            jnp.where(item_ids[None, :] == ppart[:, None], logits, jnp.float32(0.0)), axis=1
        )
        return (carry, (top, total, pos_logit))

    _, (top_loc, sum_loc, pos_loc) = lax.scan(forward, 0, (ublocks, pblocks))
    top_loc = top_loc.reshape(rows)
    sum_loc = sum_loc.reshape(rows)
    pos_loc = pos_loc.reshape(rows)
    top_all = lax.pmax(top_loc, "bank")
    sum_all = lax.psum(sum_loc * jnp.exp(top_loc - top_all), "bank")
    lse = top_all + jnp.log(sum_all)
    loss_part = jnp.sum(weight * lse) / jnp.float32(bank_size) - jnp.sum(weight * pos_loc)
    loss = lax.psum(loss_part, ("bank", "grp")) / jnp.float32(total_users)
    wblocks = weight.reshape(count, block)
    lblocks = lse.reshape(count, block)
    empty = jnp.zeros((items_here, gathered.shape[1]), jnp.float32)

    def backward(bacc, parts):
        upart, ppart, wpart, lpart = parts
        dlogits = make_dlogits(upart, ppart, wpart, lpart, bank)
        ugrad = jnp.dot(dlogits, bank, preferred_element_type=jnp.float32)
        bacc = bacc + lax.dot_general(
            dlogits, upart, (((0,), (0,)), ((), ())), preferred_element_type=jnp.float32
        )
        return (bacc, ugrad)

    bank_part, ugrads = lax.scan(backward, empty, (ublocks, pblocks, wblocks, lblocks))
    user_grad = lax.psum_scatter(
        ugrads.reshape(rows, gathered.shape[1]).astype(jnp.bfloat16),
        "bank",
        scatter_dimension=0,
        tiled=True,
    ).astype(jnp.float32)
    bank_grad = lax.psum_scatter(
        bank_part.astype(jnp.bfloat16), "grp", scatter_dimension=0, tiled=True
    ).astype(jnp.float32)
    return (loss, user_grad, bank_grad)


def solution(mesh):
    placed = (P(("bank", "grp"), None), P("bank", None), P(("bank", "grp")), P(("bank", "grp")))
    return jax.shard_map(
        per_device,
        mesh=mesh,
        in_specs=placed,
        out_specs=(P(), P(("bank", "grp"), None), P(("bank", "grp"), None)),
        check_vma=False,
    )
```

profile of v0, /device:TPU:0, one launch (start us, length us, event | category | flops | bytes accessed | tf_op | source)
XLA Modules:
  0.0 254.8 jit_solution(5209319706472410693)
XLA Ops:
  7.3 0.6 copy-done.3
  8.0 42.0 %psum.21 = f32[16]{0:T(128)S(1)} all-reduce(f32[16]{0:T(128)S(1)} %convert_reduce_fusion), channel_id=1, replica_groups=mesh['bank'=8,'grp'=4] {'bank','grp'}, use_global_device_ids=true, to_apply=%region_1.0 | all-reduce | flops 16 | bytes 128 | tf_op jit(solution)/shard_map/psum | solution.py:24
  50.0 0.7 copy-done.2
  50.7 20.2 %all-gather.1 = s32[8,1,128]{2,1,0:T(1,128)S(1)} all-gather(s32[1,1,128]{2,1,0:T(1,128)S(1)} %bitcast.82), channel_id=1, replica_groups=mesh['bank'=8,'grp'=4] {'bank'}, dimensions={0}, use_global_device_ids=true | all-gather | bytes 4608 | tf_op jit(solution)/shard_map/all_gather | solution.py:27
  70.8 16.3 %all-gather = s32[8,1,128]{2,1,0:T(1,128)S(1)} all-gather(s32[1,1,128]{2,1,0:T(1,128)S(1)} %bitcast.83), channel_id=1, replica_groups=mesh['bank'=8,'grp'=4] {'bank'}, dimensions={0}, use_global_device_ids=true | all-gather | bytes 4608 | tf_op jit(solution)/shard_map/all_gather | solution.py:28
  87.1 31.5 %all_gather.10 = bf16[1024,256]{1,0:T(8,128)(2,1)S(1)} all-gather(bf16[128,256]{1,0:T(8,128)(2,1)} %param.8), channel_id=1, replica_groups=mesh['bank'=8,'grp'=4] {'bank'}, dimensions={0}, use_global_device_ids=true | all-gather | bytes 589824 | tf_op jit(solution)/shard_map/all_gather | solution.py:26
  118.7 1.6 while.28
  118.7 0.4 fusion.34
  119.5 0.4 fusion.34
  120.3 19.3 %pmax.7 = f32[1024]{0:T(1024)S(1)} all-reduce(f32[1024]{0:T(1024)S(1)} %bitcast.76), channel_id=1, replica_groups=mesh['bank'=8,'grp'=4] {'bank'}, use_global_device_ids=true, to_apply=%region_8.9 | all-reduce | flops 1024 | bytes 8192 | tf_op jit(solution)/shard_map/pmax | solution.py:56
  139.6 17.1 %psum.22 = f32[1024]{0:T(1024)S(1)} all-reduce(f32[1024]{0:T(1024)S(1)} %exponential_multiply_fusion), channel_id=1, replica_groups=mesh['bank'=8,'grp'=4] {'bank'}, use_global_device_ids=true, to_apply=%region_9.10 | all-reduce | flops 1024 | bytes 8192 | tf_op jit(solution)/shard_map/psum | solution.py:57
  156.8 0.6 multiply_reduce_fusion.1
  157.4 2.5 while.29
  157.5 0.5 fusion.41
  157.9 0.4 convolution_add_fusion.2
  158.7 0.5 fusion.41
  159.2 0.4 convolution_add_fusion.2
  160.0 0.8 convert_element_type.28
  160.9 0.7 reduce-scatter.3.cloned.1.call-update
  162.2 0.6 multiply_reduce_fusion
  163.5 37.6 %psum.23 = f32[]{:T(128)} all-reduce(f32[]{:T(128)S(6)} %sub.36), channel_id=1, replica_groups=mesh['bank'=8,'grp'=4] {'bank','grp'}, use_global_device_ids=true, to_apply=%region_12.13 | all-reduce | flops 1 | bytes 8 | tf_op jit(solution)/shard_map/psum | solution.py:60
  201.7 1.5 convert_element_type.29
  203.3 42.1 %reduce-scatter.3.cloned.1.call-done = bf16[128,256]{1,0:T(8,128)(2,1)} async-done(((bf16[1024,256]{1,0:T(8,128)(2,1)}), bf16[128,256]{1,0:T(8,128)(2,1)}) %reduce-scatter.3.cloned.1.call-update) | async-done | bytes 65552 | tf_op jit(solution)/shard_map/reduce_scatter | solution.py:75
  245.3 1.5 convert_element_type.27
  (40 shorter events, 1.9 us)
Async XLA Ops:
  7.2 194.6 %reduce-scatter.5.cloned.1.call-start = ((), (), s32[]{:S(2)}) async-start(), calls=%async_computation.3 | async-start | bytes 327680 | tf_op jit(solution)/shard_map/reduce_scatter | solution.py:81
  7.2 0.7 copy-start.3
  50.0 0.7 copy-start.2
  87.1 31.5 %copy-start = (bf16[512,256]{1,0:T(8,128)(2,1)S(1)}, bf16[512,256]{1,0:T(8,128)(2,1)}, u32[]{:S(2)}) copy-start(bf16[512,256]{1,0:T(8,128)(2,1)} %param.9) | copy-start | bytes 786436
  160.0 0.9 copy-start.1
  160.8 84.5 %reduce-scatter.3.cloned.1.call-start = ((), (), s32[]{:S(2)}) async-start(), calls=%async_computation.2 | async-start | bytes 589824 | tf_op jit(solution)/shard_map/reduce_scatter | solution.py:75
Sparse Core Ops, SparseCore 0:
  160.9 17.9 reduce-scatter.4
  182.3 62.9 reduce-scatter.2
where the time goes:
time: 255 us
  blocking collectives  184 us (72%)
  waiting for transfers between devices  42.8 us (17%)
  between operations  17.2 us (7%)
  other arithmetic  5.83 us (2%)
  matrix products  3.1 us (1%)
    reduce_scatter x1, waiting for transfers between devices, per_device(): lax.psum_scatter(ugrads.reshape(rows, gathered.shape[1]).astype(jnp.bfloa...  42.1 us
    psum x1, blocking collectives, per_device(): counts = lax.psum(local_counts, ('bank', 'grp'))  42 us
    psum x1, blocking collectives, per_device(): loss = lax.psum(loss_part, ('bank', 'grp')) / jnp.float32(total_users)  37.6 us
    all_gather x1, blocking collectives, per_device(): lax.all_gather(users, 'bank', axis=0, tiled=True)  31.5 us
    all_gather x1, blocking collectives, per_device(): lax.all_gather(positives, 'bank', axis=0, tiled=True)  20.2 us
    pmax x1, blocking collectives, per_device(): top_all = lax.pmax(top_loc, 'bank')  19.3 us
    psum x1, blocking collectives, per_device(): sum_all = lax.psum(sum_loc * jnp.exp(top_loc - top_all), 'bank')  17.1 us
    all_gather x1, blocking collectives, per_device(): lax.all_gather(cohorts, 'bank', axis=0, tiled=True)  16.3 us
  transfers between devices with their start and end apart: 2, of which 1 were waited for; matrix products, arithmetic and copies ran while one was open for 1% of the time, Pallas kernels for 0%

commit v1 on v0

v1 whole, which is shorter than its diff:
```python
import functools

import jax
import jax.numpy as jnp
from jax import lax
from jax.experimental import pallas as pl
from jax.experimental.pallas import tpu as pltpu
from jax.sharding import PartitionSpec as P

NCOH = 16
MESH = pl.DeviceIdType.MESH
F32 = jnp.float32
BF16 = jnp.bfloat16


def kernel(
    nz, ng, users_ref, bank_ref, pos_ref, coh_ref,
    loss_ref, ug_ref, bg_ref,
    allu, pbank, meta_own, meta, ex, dl,
    loc_max, loc_sum, loc_pos, stat, posl, cw, wt,
    hist, loss_buf, ug_send, ug_recv, bg_send, bg_recv,
    bank_sem, us, ur, ms, mr, ss, sr, ps, pr, gs, gr, hs, hr, ls, lr, bs, br,
):
    per_dev = users_ref.shape[0]
    items = bank_ref.shape[0]
    share = items // ng
    nq = 2 * ng
    me_b, me_g = lax.axis_index("bank"), lax.axis_index("grp")
    zc, par = me_b // 2, me_b % 2
    me_q = par * ng + me_g

    def col_id(z):
        return {"bank": 2 * z + par, "grp": me_g}

    def plane_id(q):
        return {"bank": 2 * zc + q // ng, "grp": q % ng}

    def col(k):
        return lax.rem(zc + k, nz)

    def plane(k):
        return lax.rem(me_q + k, nq)

    def rcopy(src, dst, send, recv, dev):
        return pltpu.make_async_remote_copy(
            src_ref=src, dst_ref=dst, send_sem=send, recv_sem=recv,
            device_id=dev, device_id_type=MESH,
        )

    def rows(z):
        return pl.ds(pl.multiple_of(z * per_dev, per_dev), per_dev)

    def users_cp(k, z, slot):
        return rcopy(users_ref, allu.at[rows(slot)], us.at[k], ur.at[slot], col_id(z))

    def meta_cp(k, z, slot):
        return rcopy(meta_own, meta.at[slot], ms.at[k], mr.at[slot], col_id(z))

    def stat_cp(k, z, slot):
        return rcopy(stat.at[zc], stat.at[slot], ss.at[k], sr.at[slot], col_id(z))

    def posl_cp(k, z, slot):
        return rcopy(posl.at[zc], posl.at[slot], ps.at[k], pr.at[slot], col_id(z))

    def ug_cp(k, z, slot):
        return rcopy(ug_send.at[k], ug_recv.at[slot], gs.at[k], gr.at[slot], col_id(z))

    def hist_cp(k, q, slot):
        return rcopy(hist.at[me_q], hist.at[slot], hs.at[k], hr.at[slot], plane_id(q))

    def loss_cp(k, q, slot):
        return rcopy(loss_buf.at[me_q], loss_buf.at[slot], ls.at[k], lr.at[slot], plane_id(q))

    def bg_cp(k, q, slot):
        return rcopy(bg_send.at[k], bg_recv.at[slot], bs.at[k], br.at[slot], plane_id(q))

    bank_cp = rcopy(
        bank_ref, pbank, bank_sem.at[0], bank_sem.at[1],
        {"bank": 2 * zc + 1 - par, "grp": me_g},
    )

    barrier = pltpu.get_barrier_semaphore()
    for k in range(1, nz):
        pl.semaphore_signal(barrier, inc=1, device_id=col_id(col(k)), device_id_type=MESH)
    for k in range(1, nq):
        pl.semaphore_signal(barrier, inc=1, device_id=plane_id(plane(k)), device_id_type=MESH)

    top_rows = lax.broadcasted_iota(jnp.int32, (8, per_dev), 0) == 0
    own_meta = jnp.where(top_rows, pos_ref[...], coh_ref[...])
    meta_own[...] = own_meta
    meta[zc] = own_meta
    allu[rows(zc), :] = users_ref[...]
    item_ids = lax.broadcasted_iota(jnp.int32, (items, per_dev), 0)
    banks = (bank_ref, pbank)
    base = (me_b * items, (2 * zc + 1 - par) * items)

    def hot_of(h, z):
        return item_ids == meta[z, 0:1, :] - base[h]

    def block(h, z):
        logits = lax.dot_general(
            banks[h][...], allu[rows(z), :], (((1,), (1,)), ((), ())),
            preferred_element_type=F32,
        )
        top = jnp.max(logits, axis=0, keepdims=True)
        e = jnp.exp(logits - top)
        ex[h, z] = e
        loc_max[h, pl.ds(z, 1), :] = top
        loc_sum[h, pl.ds(z, 1), :] = jnp.sum(e, axis=0, keepdims=True)
        loc_pos[h, pl.ds(z, 1), :] = jnp.sum(
            jnp.where(hot_of(h, z), logits, F32(0.0)), axis=0, keepdims=True
        )

    pl.semaphore_wait(barrier, nz - 1 + nq - 1)
    for k in range(1, nz):
        meta_cp(k, col(k), zc).start()
    for k in range(1, nz):
        users_cp(k, col(k), zc).start()
    bank_cp.start()
    block(0, zc)

    coh_ids = lax.broadcasted_iota(jnp.int32, (NCOH, per_dev), 0)
    for k in range(1, nz):
        z = col(nz - k)
        meta_cp(k, z, z).wait_recv()

    def count(z, acc):
        return acc + (coh_ids == meta[z, 1:2, :]).astype(F32)

    hist[me_q] = lax.fori_loop(0, nz, count, jnp.zeros((NCOH, per_dev), F32))
    for k in range(1, nq):
        hist_cp(k, plane(k), me_q).start()

    def first_half(k, carry):
        z = col(nz - k)
        users_cp(k, z, z).wait_recv()
        block(0, z)
        return carry

    lax.fori_loop(1, nz, first_half, 0)
    bank_cp.wait_recv()

    def second_half(z, carry):
        block(1, z)
        return carry

    lax.fori_loop(0, nz, second_half, 0)

    m0, m1 = loc_max[0], loc_max[1]
    m = jnp.maximum(m0, m1)
    s = loc_sum[0] * jnp.exp(m0 - m) + loc_sum[1] * jnp.exp(m1 - m)
    stat[zc, 0:nz, :] = m
    stat[zc, nz : 2 * nz, :] = s
    posl[zc] = jnp.zeros(posl.shape[1:], F32)
    posl[zc, 0:nz, :] = loc_pos[0] + loc_pos[1]
    for k in range(1, nz):
        stat_cp(k, col(k), zc).start()
    for k in range(1, nz):
        posl_cp(k, col(k), zc).start()

    for k in range(1, nq):
        q = plane(nq - k)
        hist_cp(k, q, q).wait_recv()
    total = hist[0]
    for q in range(1, nq):
        total = total + hist[q]
    counts = jnp.sum(total, axis=1, keepdims=True)
    scale = F32(per_dev * nz * nq) / NCOH

    def weigh(z, carry):
        own = jnp.sum(
            jnp.where(coh_ids == meta[z, 1:2, :], counts, F32(0.0)), axis=0, keepdims=True
        )
        wt[pl.ds(z, 1), :] = scale / own
        return carry

    lax.fori_loop(0, nz, weigh, 0)
    for k in range(1, nz):
        z = col(nz - k)
        stat_cp(k, z, z).wait_recv()
    top = stat[0, 0:nz, :]
    for z in range(1, nz):
        top = jnp.maximum(top, stat[z, 0:nz, :])
    tot = jnp.zeros_like(top)
    for z in range(nz):
        tot = tot + stat[z, nz : 2 * nz, :] * jnp.exp(stat[z, 0:nz, :] - top)
    lse = top + jnp.log(tot)
    cw[0] = wt[...] * jnp.exp(m0 - lse)
    cw[1] = wt[...] * jnp.exp(m1 - lse)

    def user_term(z):
        term = None
        for h in range(2):
            w = wt[pl.ds(z, 1), :]
            d = ex[h, z] * cw[h, pl.ds(z, 1), :] - jnp.where(hot_of(h, z), w, F32(0.0))
            d = d.astype(BF16)
            dl[h, :, rows(z)] = d
            part = lax.dot_general(
                d, banks[h][...], (((0,), (0,)), ((), ())), preferred_element_type=F32
            )
            term = part if term is None else term + part
        return term.astype(BF16)

    def peers_term(k, carry):
        z = col(k)
        ug_send[k] = user_term(z)
        ug_cp(k, z, zc).start()
        return carry

    lax.fori_loop(1, nz, peers_term, 0)
    ug_recv[zc] = user_term(zc)

    def bank_term(h, g):
        left = dl[h, pl.ds(pl.multiple_of(g * share, share), share), :]
        return jnp.dot(left, allu[...], preferred_element_type=F32).astype(BF16)

    for i in range(ng):
        g = lax.rem(me_g + i, ng)
        bg_send[i] = bank_term(1, g)
        bg_cp(i, (1 - par) * ng + g, me_q).start()
    for i in range(1, ng):
        g = lax.rem(me_g + i, ng)
        bg_send[ng + i] = bank_term(0, g)
        bg_cp(ng + i, par * ng + g, me_q).start()
    bg_recv[me_q] = bank_term(0, me_g)

    for k in range(1, nz):
        z = col(nz - k)
        posl_cp(k, z, z).wait_recv()
    pos = posl[0, 0:nz, :]
    for z in range(1, nz):
        pos = pos + posl[z, 0:nz, :]
    part = jnp.sum(wt[...] * (lse - pos), axis=0, keepdims=True)
    loss_buf[me_q] = jnp.broadcast_to(part, (8, per_dev))
    for k in range(1, nq):
        loss_cp(k, plane(k), me_q).start()

    for k in range(1, nz):
        z = col(nz - k)
        ug_cp(k, z, z).wait_recv()
    acc = ug_recv[0].astype(F32)
    for z in range(1, nz):
        acc = acc + ug_recv[z].astype(F32)
    ug_ref[...] = acc
    for k in range(1, nq):
        q = plane(nq - k)
        bg_cp(k, q, q).wait_recv()
    acc = bg_recv[0].astype(F32)
    for q in range(1, nq):
        acc = acc + bg_recv[q].astype(F32)
    bg_ref[...] = acc
    for k in range(1, nq):
        q = plane(nq - k)
        loss_cp(k, q, q).wait_recv()
    acc = loss_buf[0, 0:1, :]
    for q in range(1, nq):
        acc = acc + loss_buf[q, 0:1, :]
    loss_ref[...] = jnp.sum(acc, axis=1, keepdims=True) / F32(per_dev * nz * nq)

    bank_cp.wait_send()
    for k in range(1, nz):
        z = col(k)
        for cp in (users_cp, meta_cp, stat_cp, posl_cp, ug_cp):
            cp(k, z, zc).wait_send()
    for k in range(1, nq):
        q = plane(k)
        for cp in (hist_cp, loss_cp):
            cp(k, q, me_q).wait_send()
    for k in range(nq):
        if k != ng:
            bg_cp(k, plane(1), me_q).wait_send()


def solution(mesh):
    n_bank, ng = mesh.shape["bank"], mesh.shape["grp"]
    nz, nq = n_bank // 2, 2 * ng

    def per_device(users, bank, positives, cohorts):
        per_dev, width = users.shape
        items = bank.shape[0]
        share = items // ng
        padded = -(-nz // 8) * 8
        dma = pltpu.SemaphoreType.DMA
        vmem = pl.BlockSpec(memory_space=pltpu.VMEM)
        loss, ug, bg = pl.pallas_call(
            functools.partial(kernel, nz, ng),
            out_shape=(
                jax.ShapeDtypeStruct((1, 1), F32),
                jax.ShapeDtypeStruct((per_dev, width), F32),
                jax.ShapeDtypeStruct((share, width), F32),
            ),
            in_specs=[vmem] * 4,
            out_specs=(vmem, vmem, vmem),
            scratch_shapes=[
                pltpu.VMEM((nz * per_dev, width), BF16),
                pltpu.VMEM((items, width), BF16),
                pltpu.VMEM((8, per_dev), jnp.int32),
                pltpu.VMEM((nz, 8, per_dev), jnp.int32),
                pltpu.VMEM((2, nz, items, per_dev), F32),
                pltpu.VMEM((2, items, nz * per_dev), BF16),
                pltpu.VMEM((2, nz, per_dev), F32),
                pltpu.VMEM((2, nz, per_dev), F32),
                pltpu.VMEM((2, nz, per_dev), F32),
                pltpu.VMEM((nz, 2 * nz, per_dev), F32),
                pltpu.VMEM((nz, padded, per_dev), F32),
                pltpu.VMEM((2, nz, per_dev), F32),
                pltpu.VMEM((nz, per_dev), F32),
                pltpu.VMEM((nq, NCOH, per_dev), F32),
                pltpu.VMEM((nq, 8, per_dev), F32),
                pltpu.VMEM((nz, per_dev, width), BF16),
                pltpu.VMEM((nz, per_dev, width), BF16),
                pltpu.VMEM((nq, share, width), BF16),
                pltpu.VMEM((nq, share, width), BF16),
                dma((2,)),
                dma((nz,)), dma((nz,)), dma((nz,)), dma((nz,)), dma((nz,)),
                dma((nz,)), dma((nz,)), dma((nz,)), dma((nz,)), dma((nz,)),
                dma((nq,)), dma((nq,)), dma((nq,)), dma((nq,)), dma((nq,)), dma((nq,)),
            ],
            compiler_params=pltpu.CompilerParams(collective_id=0, has_side_effects=True),
        )(users, bank, positives.reshape(1, per_dev), cohorts.reshape(1, per_dev))
        return loss.reshape(()), ug, bg

    placed = (P(("bank", "grp"), None), P("bank", None), P(("bank", "grp")), P(("bank", "grp")))
    return jax.shard_map(
        per_device,
        mesh=mesh,
        in_specs=placed,
        out_specs=(P(), P(("bank", "grp"), None), P(("bank", "grp"), None)),
        check_vma=False,
    )
```

time: 255 us -> 34.1 us (0.13)
  blocking collectives: 184 us -> 0 us
  waiting for transfers between devices: 42.8 us -> 0 us
  Pallas kernels: 0 us -> 29.3 us
  between operations: 17.2 us -> 2.32 us
  other arithmetic: 5.83 us -> 0 us
  matrix products: 3.1 us -> 0 us
    psum x3 -> x0, blocking collectives: 96.7 us -> none  [the longest x1 42 us: per_device(): counts = lax.psum(local_counts, ('bank', 'grp'))]
    all_gather x3 -> x0, blocking collectives: 68 us -> none  [the longest x1 31.5 us: per_device(): lax.all_gather(users, 'bank', axis=0, tiled=True)]
    reduce_scatter x2 -> x0, waiting for transfers between devices: 42.1 us -> none  [the longest x1 42.1 us: per_device(): lax.psum_scatter(ugrads.reshape(rows, gathered.shape[1]).astype(jnp.bfloa...]
    pallas_call x0 -> x1, Pallas kernels: none -> 29.3 us  [per_device(): pl.pallas_call(functools.partial(kernel, nz, ng), out_shape=(jax.ShapeDty...]
    pmax x1 -> x0, blocking collectives: 19.3 us -> none  [per_device(): top_all = lax.pmax(top_loc, 'bank')]
    convert_element_type x3 -> x0, other arithmetic: 3.8 us -> none  [the longest x1 1.51 us: per_device(): bank_grad = lax.psum_scatter(bank_part.astype(jnp.bfloat16), 'grp', scatt...]
    dot_general x8 -> x0, matrix products: 3.1 us -> none  [the longest x2 0.91 us: make_dlogits(): logits = jnp.dot(upart, bank.T, preferred_element_type=jnp.float32)]
  transfers between devices with their start and end apart: 2 -> 0, of which waited for: 1 -> 0; matrix products, arithmetic and copies ran while one was open for 1% -> 0% of each run, Pallas kernels for 0% -> 0%
where the time goes in v1:
time: 34.1 us; the launch traced here: 33.9 us
  Pallas kernels  29.3 us (86%)
  between operations  2.32 us (7%)
  local copies, waits for them, and re-layouts  2.26 us (7%)
    pallas_call x1, Pallas kernels, per_device(): pl.pallas_call(functools.partial(kernel, nz, ng), out_shape=(jax.ShapeDty...  29.3 us
    unnamed x4, local copies, waits for them, and re-layouts  2.26 us

profile of v1, /device:TPU:0, one launch (start us, length us, event | category | flops | bytes accessed | tf_op | source)
XLA Modules:
  0.0 33.9 jit_solution(7348484186584248925)
XLA Ops:
  0.6 29.3 %shard_map.67 = (f32[1,1]{1,0:T(1,128)}, f32[128,256]{1,0:T(8,128)}, f32[128,256]{1,0:T(8,128)}) custom-call(bf16[128,256]{1,0:T(8,128)(2,1)} %users_ref.1, bf16[512,256]{1,0:T(8,128)(2,1)} %bank_ref.1, s32[1,128]{1,0:T(1,128)} %bitcast.3, s32[1,128]{1,0:T(1,128)} %bitcast.4), custom_call_target="tpu_custom_call" | custom-call | tf_op jit(solution)/shard_map/pallas_call | solution.py:285
  30.5 0.0 copy-start
  30.5 1.6 %copy.11 = f32[128,256]{1,0:T(8,128)} copy(f32[128,256]{1,0:T(8,128)} %get-tuple-element.13) | data formatting | bytes 262144
  32.1 0.0 copy-done
  32.1 0.7 %copy.12 = f32[128,256]{1,0:T(8,128)} copy(f32[128,256]{1,0:T(8,128)S(1)} %copy-done) | data formatting | bytes 262144
Async XLA Ops:
  30.5 1.6 %copy-start = (f32[128,256]{1,0:T(8,128)S(1)}, f32[128,256]{1,0:T(8,128)}, u32[]{:S(2)}) copy-start(f32[128,256]{1,0:T(8,128)} %get-tuple-element.14) | copy-start | bytes 393220

commit v2 on v1

--- a/solution.py
+++ b/solution.py
@@ -14,15 +14,15 @@
 
 
 def kernel(
-    nz, ng, users_ref, bank_ref, pos_ref, coh_ref,
-    loss_ref, ug_ref, bg_ref,
-    allu, pbank, meta_own, meta, ex, dl,
+    nz, ng, users_hbm, bank_hbm, pos_hbm, coh_hbm,
+    loss_buf, ug_recv, bg_recv,
+    allu, bank_ref, pbank, pos_ref, coh_ref, local, meta_own, meta, ex, dl,
     loc_max, loc_sum, loc_pos, stat, posl, cw, wt,
-    hist, loss_buf, ug_send, ug_recv, bg_send, bg_recv,
+    hist, ug_send, bg_send,
     bank_sem, us, ur, ms, mr, ss, sr, ps, pr, gs, gr, hs, hr, ls, lr, bs, br,
 ):
-    per_dev = users_ref.shape[0]
-    items = bank_ref.shape[0]
+    per_dev = users_hbm.shape[0]
+    items = bank_hbm.shape[0]
     share = items // ng
     nq = 2 * ng
     me_b, me_g = lax.axis_index("bank"), lax.axis_index("grp")
@@ -36,7 +36,11 @@
         return {"bank": 2 * zc + q // ng, "grp": q % ng}
 
     def col(k):
-        return lax.rem(zc + k, nz)
+        down, up = nz - k, k - 1
+        down = down - (zc - down + nz) // nz
+        up = up + (up - zc + nz) // nz
+        upper = (2 * zc) // nz
+        return (1 - upper) * down + upper * up
 
     def plane(k):
         return lax.rem(me_q + k, nq)
@@ -51,7 +55,7 @@
         return pl.ds(pl.multiple_of(z * per_dev, per_dev), per_dev)
 
     def users_cp(k, z, slot):
-        return rcopy(users_ref, allu.at[rows(slot)], us.at[k], ur.at[slot], col_id(z))
+        return rcopy(allu.at[rows(zc)], allu.at[rows(slot)], us.at[k], ur.at[slot], col_id(z))
 
     def meta_cp(k, z, slot):
         return rcopy(meta_own, meta.at[slot], ms.at[k], mr.at[slot], col_id(z))
@@ -85,11 +89,21 @@
     for k in range(1, nq):
         pl.semaphore_signal(barrier, inc=1, device_id=plane_id(plane(k)), device_id_type=MESH)
 
+    loads = [
+        pltpu.make_async_copy(src, dst, local.at[i])
+        for i, (src, dst) in enumerate((
+            (pos_hbm, pos_ref), (coh_hbm, coh_ref),
+            (users_hbm, allu.at[rows(zc)]), (bank_hbm, bank_ref),
+        ))
+    ]
+    for load in loads:
+        load.start()
+    for load in loads[:2]:
+        load.wait()
     top_rows = lax.broadcasted_iota(jnp.int32, (8, per_dev), 0) == 0
     own_meta = jnp.where(top_rows, pos_ref[...], coh_ref[...])
     meta_own[...] = own_meta
     meta[zc] = own_meta
-    allu[rows(zc), :] = users_ref[...]
     item_ids = lax.broadcasted_iota(jnp.int32, (items, per_dev), 0)
     banks = (bank_ref, pbank)
     base = (me_b * items, (2 * zc + 1 - par) * items)
@@ -111,6 +125,8 @@
             jnp.where(hot_of(h, z), logits, F32(0.0)), axis=0, keepdims=True
         )
 
+    for load in loads[2:]:
+        load.wait()
     pl.semaphore_wait(barrier, nz - 1 + nq - 1)
     for k in range(1, nz):
         meta_cp(k, col(k), zc).start()
@@ -131,20 +147,17 @@
     for k in range(1, nq):
         hist_cp(k, plane(k), me_q).start()
 
-    def first_half(k, carry):
+    bank_cp.wait_recv()
+    block(1, zc)
+
+    def arriving(k, carry):
         z = col(nz - k)
         users_cp(k, z, z).wait_recv()
         block(0, z)
-        return carry
-
-    lax.fori_loop(1, nz, first_half, 0)
-    bank_cp.wait_recv()
-
-    def second_half(z, carry):
         block(1, z)
         return carry
 
-    lax.fori_loop(0, nz, second_half, 0)
+    lax.fori_loop(1, nz, arriving, 0)
 
     m0, m1 = loc_max[0], loc_max[1]
     m = jnp.maximum(m0, m1)
@@ -188,27 +201,32 @@
     cw[0] = wt[...] * jnp.exp(m0 - lse)
     cw[1] = wt[...] * jnp.exp(m1 - lse)
 
+    def dlogits(h, z):
+        w = wt[pl.ds(z, 1), :]
+        d = ex[h, z] * cw[h, pl.ds(z, 1), :] - jnp.where(hot_of(h, z), w, F32(0.0))
+        dl[h, :, rows(z)] = d.astype(BF16)
+
     def user_term(z):
         term = None
         for h in range(2):
-            w = wt[pl.ds(z, 1), :]
-            d = ex[h, z] * cw[h, pl.ds(z, 1), :] - jnp.where(hot_of(h, z), w, F32(0.0))
-            d = d.astype(BF16)
-            dl[h, :, rows(z)] = d
             part = lax.dot_general(
-                d, banks[h][...], (((0,), (0,)), ((), ())), preferred_element_type=F32
+                dl[h, :, rows(z)], banks[h][...], (((0,), (0,)), ((), ())),
+                preferred_element_type=F32,
             )
             term = part if term is None else term + part
         return term.astype(BF16)
 
     def peers_term(k, carry):
         z = col(k)
+        dlogits(0, z)
+        dlogits(1, z)
         ug_send[k] = user_term(z)
         ug_cp(k, z, zc).start()
         return carry
 
     lax.fori_loop(1, nz, peers_term, 0)
-    ug_recv[zc] = user_term(zc)
+    dlogits(0, zc)
+    dlogits(1, zc)
 
     def bank_term(h, g):
         left = dl[h, pl.ds(pl.multiple_of(g * share, share), share), :]
@@ -223,6 +241,7 @@
         bg_send[ng + i] = bank_term(0, g)
         bg_cp(ng + i, par * ng + g, me_q).start()
     bg_recv[me_q] = bank_term(0, me_g)
+    ug_recv[zc] = user_term(zc)
 
     for k in range(1, nz):
         z = col(nz - k)
@@ -238,24 +257,12 @@
     for k in range(1, nz):
         z = col(nz - k)
         ug_cp(k, z, z).wait_recv()
-    acc = ug_recv[0].astype(F32)
-    for z in range(1, nz):
-        acc = acc + ug_recv[z].astype(F32)
-    ug_ref[...] = acc
     for k in range(1, nq):
         q = plane(nq - k)
         bg_cp(k, q, q).wait_recv()
-    acc = bg_recv[0].astype(F32)
-    for q in range(1, nq):
-        acc = acc + bg_recv[q].astype(F32)
-    bg_ref[...] = acc
     for k in range(1, nq):
         q = plane(nq - k)
         loss_cp(k, q, q).wait_recv()
-    acc = loss_buf[0, 0:1, :]
-    for q in range(1, nq):
-        acc = acc + loss_buf[q, 0:1, :]
-    loss_ref[...] = jnp.sum(acc, axis=1, keepdims=True) / F32(per_dev * nz * nq)
 
     bank_cp.wait_send()
     for k in range(1, nz):
@@ -269,6 +276,23 @@
     for k in range(nq):
         if k != ng:
             bg_cp(k, plane(1), me_q).wait_send()
+
+
+def finish(users, loss_buf, ug_recv, bg_recv, loss_ref, ug_hbm, bg_hbm, ug, bg, sem):
+    copies = []
+    for i, (terms, total, out) in enumerate(((ug_recv, ug, ug_hbm), (bg_recv, bg, bg_hbm))):
+        acc = terms[0].astype(F32)
+        for t in range(1, terms.shape[0]):
+            acc = acc + terms[t].astype(F32)
+        total[...] = acc
+        copies.append(pltpu.make_async_copy(total, out, sem.at[i]))
+        copies[-1].start()
+    acc = loss_buf[0, 0:1, :]
+    for q in range(1, loss_buf.shape[0]):
+        acc = acc + loss_buf[q, 0:1, :]
+    loss_ref[...] = jnp.sum(acc, axis=1, keepdims=True) / F32(users)
+    for copy in copies:
+        copy.wait()
 
 
 def solution(mesh):
@@ -282,18 +306,23 @@
         padded = -(-nz // 8) * 8
         dma = pltpu.SemaphoreType.DMA
         vmem = pl.BlockSpec(memory_space=pltpu.VMEM)
-        loss, ug, bg = pl.pallas_call(
+        anywhere = pl.BlockSpec(memory_space=pl.ANY)
+        received = pl.pallas_call(
             functools.partial(kernel, nz, ng),
             out_shape=(
-                jax.ShapeDtypeStruct((1, 1), F32),
-                jax.ShapeDtypeStruct((per_dev, width), F32),
-                jax.ShapeDtypeStruct((share, width), F32),
+                pltpu.VMEM((nq, 8, per_dev), F32),
+                pltpu.VMEM((nz, per_dev, width), BF16),
+                pltpu.VMEM((nq, share, width), BF16),
             ),
-            in_specs=[vmem] * 4,
+            in_specs=[anywhere] * 4,
             out_specs=(vmem, vmem, vmem),
             scratch_shapes=[
                 pltpu.VMEM((nz * per_dev, width), BF16),
                 pltpu.VMEM((items, width), BF16),
+                pltpu.VMEM((items, width), BF16),
+                pltpu.VMEM((1, per_dev), jnp.int32),
+                pltpu.VMEM((1, per_dev), jnp.int32),
+                dma((4,)),
                 pltpu.VMEM((8, per_dev), jnp.int32),
                 pltpu.VMEM((nz, 8, per_dev), jnp.int32),
                 pltpu.VMEM((2, nz, items, per_dev), F32),
@@ -306,10 +335,7 @@
                 pltpu.VMEM((2, nz, per_dev), F32),
                 pltpu.VMEM((nz, per_dev), F32),
                 pltpu.VMEM((nq, NCOH, per_dev), F32),
-                pltpu.VMEM((nq, 8, per_dev), F32),
                 pltpu.VMEM((nz, per_dev, width), BF16),
-                pltpu.VMEM((nz, per_dev, width), BF16),
-                pltpu.VMEM((nq, share, width), BF16),
                 pltpu.VMEM((nq, share, width), BF16),
                 dma((2,)),
                 dma((nz,)), dma((nz,)), dma((nz,)), dma((nz,)), dma((nz,)),
@@ -318,6 +344,21 @@
             ],
             compiler_params=pltpu.CompilerParams(collective_id=0, has_side_effects=True),
         )(users, bank, positives.reshape(1, per_dev), cohorts.reshape(1, per_dev))
+        loss, ug, bg = pl.pallas_call(
+            functools.partial(finish, per_dev * nz * nq),
+            out_shape=(
+                jax.ShapeDtypeStruct((1, 1), F32),
+                jax.ShapeDtypeStruct((per_dev, width), F32),
+                jax.ShapeDtypeStruct((share, width), F32),
+            ),
+            in_specs=[vmem] * 3,
+            out_specs=(vmem, anywhere, anywhere),
+            scratch_shapes=[
+                pltpu.VMEM((per_dev, width), F32),
+                pltpu.VMEM((share, width), F32),
+                dma((2,)),
+            ],
+        )(*(pltpu.with_memory_space_constraint(x, pltpu.VMEM) for x in received))
         return loss.reshape(()), ug, bg
 
     placed = (P(("bank", "grp"), None), P("bank", None), P(("bank", "grp")), P(("bank", "grp")))

time: 34.1 us -> 29.9 us (0.88)
  local copies, waits for them, and re-layouts: 2.26 us -> 0 us
  between operations: 2.32 us -> 0.64 us
    unnamed x4 -> x0, local copies, waits for them, and re-layouts: 2.26 us -> none
    pallas_call x1 -> x2, Pallas kernels: 29.3 us -> 29.1 us  [the longest x1 27.8 us: per_device(): pl.pallas_call(functools.partial(kernel, nz, ng), out_shape=(pltpu.VMEM((...]
where the time goes in v2:
time: 29.9 us; the launch traced here: 29.7 us
  Pallas kernels  29.1 us (97%)
  between operations  0.64 us (2%)
    pallas_call x1, Pallas kernels, per_device(): pl.pallas_call(functools.partial(kernel, nz, ng), out_shape=(pltpu.VMEM((...  27.8 us
    pallas_call x1, Pallas kernels, per_device(): pl.pallas_call(functools.partial(finish, per_dev * nz * nq), out_shape=(j...  1.3 us

profile of v2, /device:TPU:0, one launch (start us, length us, event | category | flops | bytes accessed | tf_op | source)
XLA Modules:
  0.0 29.7 jit_solution(9122568622507800960)
XLA Ops:
  0.6 27.8 %shard_map.67 = (f32[8,8,128]{2,1,0:T(8,128)S(1)}, bf16[4,128,256]{2,1,0:T(8,128)(2,1)S(1)}, bf16[8,128,256]{2,1,0:T(8,128)(2,1)S(1)}) custom-call(bf16[128,256]{1,0:T(8,128)(2,1)} %users_hbm.1, bf16[512,256]{1,0:T(8,128)(2,1)} %bank_hbm.1, s32[1,128]{1,0:T(1,128)} %bitcast.3, s32[1,128]{1,0:T(1,128)} %bitcast.4), custom_call_target="tpu_custom_call" | custom-call | tf_op jit(solution)/shard_map/pallas_call | solution.py:310
  28.4 1.3 %shard_map.68 = (f32[1,1]{1,0:T(1,128)}, f32[128,256]{1,0:T(8,128)}, f32[128,256]{1,0:T(8,128)}) custom-call(f32[8,8,128]{2,1,0:T(8,128)S(1)} %get-tuple-element.9.loss_buf, bf16[4,128,256]{2,1,0:T(8,128)(2,1)S(1)} %get-tuple-element.10.ug_recv, bf16[8,128,256]{2,1,0:T(8,128)(2,1)S(1)} %get-tuple-element.11.bg_recv), custom_call_target="tpu_custom_call" | custom-call | tf_op jit(solution)/shard_map/pallas_call | solution.py:347

commit v3 on v2

--- a/solution.py
+++ b/solution.py
@@ -18,8 +18,8 @@
     loss_buf, ug_recv, bg_recv,
     allu, bank_ref, pbank, pos_ref, coh_ref, local, meta_own, meta, ex, dl,
     loc_max, loc_sum, loc_pos, stat, posl, cw, wt,
-    hist, ug_send, bg_send,
-    bank_sem, us, ur, ms, mr, ss, sr, ps, pr, gs, gr, hs, hr, ls, lr, bs, br,
+    hist, et, ht, ug_send, bg_send, pre_send, pre_recv,
+    bank_sem, us, ur, ms, mr, ss, sr, ps, pr, gs, gr, hs, hr, ls, lr, bs, br, xs, xr,
 ):
     per_dev = users_hbm.shape[0]
     items = bank_hbm.shape[0]
@@ -28,6 +28,11 @@
     me_b, me_g = lax.axis_index("bank"), lax.axis_index("grp")
     zc, par = me_b // 2, me_b % 2
     me_q = par * ng + me_g
+    npair, half = ng // 2, items // 2
+    pair, side = me_g // 2, me_g % 2
+    nr = 2 * npair
+    me_r = par * npair + pair
+    sibling = {"bank": me_b, "grp": 2 * pair + 1 - side}
 
     def col_id(z):
         return {"bank": 2 * z + par, "grp": me_g}
@@ -75,12 +80,27 @@
     def loss_cp(k, q, slot):
         return rcopy(loss_buf.at[me_q], loss_buf.at[slot], ls.at[k], lr.at[slot], plane_id(q))
 
-    def bg_cp(k, q, slot):
-        return rcopy(bg_send.at[k], bg_recv.at[slot], bs.at[k], br.at[slot], plane_id(q))
+    def bg_cp(k, r, slot):
+        dev = {"bank": 2 * zc + r // npair, "grp": 2 * (r % npair) + side}
+        return rcopy(bg_send.at[k], bg_recv.at[slot], bs.at[k], br.at[slot], dev)
+
+    def pre_cp(k):
+        return rcopy(pre_send.at[k], pre_recv.at[k], xs.at[k], xr.at[k], sibling)
+
+    def half_rows(i):
+        return pl.ds(pl.multiple_of(i * half, half), half)
 
     bank_cp = rcopy(
-        bank_ref, pbank, bank_sem.at[0], bank_sem.at[1],
-        {"bank": 2 * zc + 1 - par, "grp": me_g},
+        bank_ref.at[half_rows(side)], pbank.at[half_rows(side)],
+        bank_sem.at[0], bank_sem.at[1], {"bank": 2 * zc + 1 - par, "grp": me_g},
+    )
+    forward_cp = rcopy(
+        pbank.at[half_rows(side)], pbank.at[half_rows(side)],
+        bank_sem.at[2], bank_sem.at[3], sibling,
+    )
+    forwarded_cp = rcopy(
+        pbank.at[half_rows(1 - side)], pbank.at[half_rows(1 - side)],
+        bank_sem.at[2], bank_sem.at[3], sibling,
     )
 
     barrier = pltpu.get_barrier_semaphore()
@@ -130,9 +150,9 @@
     pl.semaphore_wait(barrier, nz - 1 + nq - 1)
     for k in range(1, nz):
         meta_cp(k, col(k), zc).start()
+    bank_cp.start()
     for k in range(1, nz):
         users_cp(k, col(k), zc).start()
-    bank_cp.start()
     block(0, zc)
 
     coh_ids = lax.broadcasted_iota(jnp.int32, (NCOH, per_dev), 0)
@@ -148,7 +168,13 @@
         hist_cp(k, plane(k), me_q).start()
 
     bank_cp.wait_recv()
+    forward_cp.start()
+    near = col(nz - 1)
+    users_cp(1, near, near).wait_recv()
+    block(0, near)
+    forwarded_cp.wait_recv()
     block(1, zc)
+    block(1, near)
 
     def arriving(k, carry):
         z = col(nz - k)
@@ -157,7 +183,7 @@
         block(1, z)
         return carry
 
-    lax.fori_loop(1, nz, arriving, 0)
+    lax.fori_loop(2, nz, arriving, 0)
 
     m0, m1 = loc_max[0], loc_max[1]
     m = jnp.maximum(m0, m1)
@@ -170,6 +196,21 @@
         stat_cp(k, col(k), zc).start()
     for k in range(1, nz):
         posl_cp(k, col(k), zc).start()
+
+    def turned(left, h):
+        return lax.dot_general(
+            left.astype(BF16), banks[h][...], (((0,), (0,)), ((), ())),
+            preferred_element_type=F32,
+        )
+
+    def ahead(z, carry):
+        for h in range(2):
+            et[h, z] = turned(ex[h, z], h)
+        ones = [jnp.where(hot_of(h, z), F32(1.0), F32(0.0)) for h in range(2)]
+        ht[z] = turned(ones[0], 0) + turned(ones[1], 1)
+        return carry
+
+    lax.fori_loop(0, nz, ahead, 0)
 
     for k in range(1, nq):
         q = plane(nq - k)
@@ -206,42 +247,50 @@
         d = ex[h, z] * cw[h, pl.ds(z, 1), :] - jnp.where(hot_of(h, z), w, F32(0.0))
         dl[h, :, rows(z)] = d.astype(BF16)
 
+    eight = lax.broadcasted_iota(jnp.int32, (8, per_dev), 0)
+
     def user_term(z):
-        term = None
-        for h in range(2):
-            part = lax.dot_general(
-                dl[h, :, rows(z)], banks[h][...], (((0,), (0,)), ((), ())),
-                preferred_element_type=F32,
-            )
-            term = part if term is None else term + part
+        row = pl.ds(z, 1)
+        c0, c1, w = cw[0, row, :], cw[1, row, :], wt[row, :]
+        turn = jnp.transpose(jnp.where(eight == 0, c0, jnp.where(eight == 1, c1, w)))
+        term = et[0, z] * turn[:, 0:1] + et[1, z] * turn[:, 1:2] - ht[z] * turn[:, 2:3]
         return term.astype(BF16)
 
-    def peers_term(k, carry):
+    for k in range(1, nz):
         z = col(k)
+        ug_send[k] = user_term(z)
+        ug_cp(k, z, zc).start()
+
+    def both(z, carry):
         dlogits(0, z)
         dlogits(1, z)
-        ug_send[k] = user_term(z)
-        ug_cp(k, z, zc).start()
         return carry
 
-    lax.fori_loop(1, nz, peers_term, 0)
-    dlogits(0, zc)
-    dlogits(1, zc)
+    lax.fori_loop(0, nz, both, 0)
 
     def bank_term(h, g):
         left = dl[h, pl.ds(pl.multiple_of(g * share, share), share), :]
-        return jnp.dot(left, allu[...], preferred_element_type=F32).astype(BF16)
-
-    for i in range(ng):
-        g = lax.rem(me_g + i, ng)
-        bg_send[i] = bank_term(1, g)
-        bg_cp(i, (1 - par) * ng + g, me_q).start()
-    for i in range(1, ng):
-        g = lax.rem(me_g + i, ng)
-        bg_send[ng + i] = bank_term(0, g)
-        bg_cp(ng + i, par * ng + g, me_q).start()
-    bg_recv[me_q] = bank_term(0, me_g)
+        return jnp.dot(left, allu[...], preferred_element_type=F32)
+
+    order = [(h, i) for h in (1, 0) for i in range(npair - 1, -1, -1)]
+
+    def pair_at(i):
+        return lax.rem(pair + i, npair)
+
+    for j, (h, i) in enumerate(order):
+        pre_send[j] = bank_term(h, 2 * pair_at(i) + 1 - side).astype(BF16)
+        pre_cp(j).start()
     ug_recv[zc] = user_term(zc)
+    for j, (h, i) in enumerate(order):
+        term = bank_term(h, 2 * pair_at(i) + side)
+        pre_cp(j).wait_recv()
+        term = (term + pre_recv[j].astype(F32)).astype(BF16)
+        if j < nr - 1:
+            bg_send[j] = term
+            goal = (par if h == 0 else 1 - par) * npair + pair_at(i)
+            bg_cp(j, goal, me_r).start()
+        else:
+            bg_recv[me_r] = term
 
     for k in range(1, nz):
         z = col(nz - k)
@@ -257,14 +306,15 @@
     for k in range(1, nz):
         z = col(nz - k)
         ug_cp(k, z, z).wait_recv()
-    for k in range(1, nq):
-        q = plane(nq - k)
-        bg_cp(k, q, q).wait_recv()
+    for k in range(1, nr):
+        r = lax.rem(me_r + k, nr)
+        bg_cp(k, r, r).wait_recv()
     for k in range(1, nq):
         q = plane(nq - k)
         loss_cp(k, q, q).wait_recv()
 
     bank_cp.wait_send()
+    forward_cp.wait_send()
     for k in range(1, nz):
         z = col(k)
         for cp in (users_cp, meta_cp, stat_cp, posl_cp, ug_cp):
@@ -273,9 +323,10 @@
         q = plane(k)
         for cp in (hist_cp, loss_cp):
             cp(k, q, me_q).wait_send()
-    for k in range(nq):
-        if k != ng:
-            bg_cp(k, plane(1), me_q).wait_send()
+    for j in range(nr):
+        pre_cp(j).wait_send()
+        if j < nr - 1:
+            bg_cp(j, lax.rem(me_r + 1, nr), me_r).wait_send()
 
 
 def finish(users, loss_buf, ug_recv, bg_recv, loss_ref, ug_hbm, bg_hbm, ug, bg, sem):
@@ -312,7 +363,7 @@
             out_shape=(
                 pltpu.VMEM((nq, 8, per_dev), F32),
                 pltpu.VMEM((nz, per_dev, width), BF16),
-                pltpu.VMEM((nq, share, width), BF16),
+                pltpu.VMEM((ng, share, width), BF16),
             ),
             in_specs=[anywhere] * 4,
             out_specs=(vmem, vmem, vmem),
@@ -335,12 +386,17 @@
                 pltpu.VMEM((2, nz, per_dev), F32),
                 pltpu.VMEM((nz, per_dev), F32),
                 pltpu.VMEM((nq, NCOH, per_dev), F32),
+                pltpu.VMEM((2, nz, per_dev, width), F32),
+                pltpu.VMEM((nz, per_dev, width), F32),
                 pltpu.VMEM((nz, per_dev, width), BF16),
-                pltpu.VMEM((nq, share, width), BF16),
-                dma((2,)),
+                pltpu.VMEM((ng, share, width), BF16),
+                pltpu.VMEM((ng, share, width), BF16),
+                pltpu.VMEM((ng, share, width), BF16),
+                dma((4,)),
                 dma((nz,)), dma((nz,)), dma((nz,)), dma((nz,)), dma((nz,)),
                 dma((nz,)), dma((nz,)), dma((nz,)), dma((nz,)), dma((nz,)),
-                dma((nq,)), dma((nq,)), dma((nq,)), dma((nq,)), dma((nq,)), dma((nq,)),
+                dma((nq,)), dma((nq,)), dma((nq,)), dma((nq,)),
+                dma((ng,)), dma((ng,)), dma((ng,)), dma((ng,)),
             ],
             compiler_params=pltpu.CompilerParams(collective_id=0, has_side_effects=True),
         )(users, bank, positives.reshape(1, per_dev), cohorts.reshape(1, per_dev))

time: 29.9 us -> 28.4 us (0.950)
  Pallas kernels: 29.1 us -> 27.6 us
    pallas_call x1, Pallas kernels: 27.8 us -> 26.3 us  [per_device(): pl.pallas_call(functools.partial(kernel, nz, ng), out_shape=(pltpu.VMEM((...]
where the time goes in v3:
time: 28.4 us; the launch traced here: 28.3 us
  Pallas kernels  27.6 us (97%)
  between operations  0.64 us (2%)
    pallas_call x1, Pallas kernels, per_device(): pl.pallas_call(functools.partial(kernel, nz, ng), out_shape=(pltpu.VMEM((...  26.3 us
    pallas_call x1, Pallas kernels, per_device(): pl.pallas_call(functools.partial(finish, per_dev * nz * nq), out_shape=(j...  1.27 us

profile of v3, /device:TPU:0, one launch (start us, length us, event | category | flops | bytes accessed | tf_op | source)
XLA Modules:
  0.0 28.3 jit_solution(11487912499591759881)
XLA Ops:
  0.6 26.3 %shard_map.67 = (f32[8,8,128]{2,1,0:T(8,128)S(1)}, bf16[4,128,256]{2,1,0:T(8,128)(2,1)S(1)}, bf16[4,128,256]{2,1,0:T(8,128)(2,1)S(1)}) custom-call(bf16[128,256]{1,0:T(8,128)(2,1)} %users_hbm.1, bf16[512,256]{1,0:T(8,128)(2,1)} %bank_hbm.1, s32[1,128]{1,0:T(1,128)} %bitcast.3, s32[1,128]{1,0:T(1,128)} %bitcast.4), custom_call_target="tpu_custom_call" | custom-call | tf_op jit(solution)/shard_map/pallas_call | solution.py:361
  27.0 1.3 %shard_map.68 = (f32[1,1]{1,0:T(1,128)}, f32[128,256]{1,0:T(8,128)}, f32[128,256]{1,0:T(8,128)}) custom-call(f32[8,8,128]{2,1,0:T(8,128)S(1)} %get-tuple-element.9.loss_buf, bf16[4,128,256]{2,1,0:T(8,128)(2,1)S(1)} %get-tuple-element.10.ug_recv, bf16[4,128,256]{2,1,0:T(8,128)(2,1)S(1)} %get-tuple-element.11.bg_recv), custom_call_target="tpu_custom_call" | custom-call | tf_op jit(solution)/shard_map/pallas_call | solution.py:403

commit v4 on v3

--- a/solution.py
+++ b/solution.py
@@ -147,13 +147,13 @@
 
     for load in loads[2:]:
         load.wait()
+    block(0, zc)
     pl.semaphore_wait(barrier, nz - 1 + nq - 1)
     for k in range(1, nz):
         meta_cp(k, col(k), zc).start()
     bank_cp.start()
     for k in range(1, nz):
         users_cp(k, col(k), zc).start()
-    block(0, zc)
 
     coh_ids = lax.broadcasted_iota(jnp.int32, (NCOH, per_dev), 0)
     for k in range(1, nz):
@@ -256,32 +256,49 @@
         term = et[0, z] * turn[:, 0:1] + et[1, z] * turn[:, 1:2] - ht[z] * turn[:, 2:3]
         return term.astype(BF16)
 
+    def form(h):
+        def step(z, carry):
+            dlogits(h, z)
+            return carry
+
+        lax.fori_loop(0, nz, step, 0, unroll=nz <= 4)
+
+    def bank_term(h, g):
+        left = dl[h, pl.ds(pl.multiple_of(g * share, share), share), :]
+        return jnp.dot(left, allu[...], preferred_element_type=F32)
+
+    order = [(h, i) for h in (1, 0) for i in range(npair - 1, -1, -1)]
+
+    def pair_at(i):
+        return lax.rem(pair + i, npair)
+
+    def give(j):
+        h, i = order[j]
+        pre_send[j] = bank_term(h, 2 * pair_at(i) + 1 - side).astype(BF16)
+        pre_cp(j).start()
+
+    form(1)
+    for j in range(npair):
+        give(j)
     for k in range(1, nz):
         z = col(k)
         ug_send[k] = user_term(z)
         ug_cp(k, z, zc).start()
 
-    def both(z, carry):
-        dlogits(0, z)
-        dlogits(1, z)
-        return carry
-
-    lax.fori_loop(0, nz, both, 0)
-
-    def bank_term(h, g):
-        left = dl[h, pl.ds(pl.multiple_of(g * share, share), share), :]
-        return jnp.dot(left, allu[...], preferred_element_type=F32)
-
-    order = [(h, i) for h in (1, 0) for i in range(npair - 1, -1, -1)]
-
-    def pair_at(i):
-        return lax.rem(pair + i, npair)
-
+    for k in range(1, nz):
+        z = col(nz - k)
+        posl_cp(k, z, z).wait_recv()
+    pos = posl[0, 0:nz, :]
+    for z in range(1, nz):
+        pos = pos + posl[z, 0:nz, :]
+    part = jnp.sum(wt[...] * (lse - pos), axis=0, keepdims=True)
+    loss_buf[me_q] = jnp.broadcast_to(part, (8, per_dev))
+    for k in range(1, nq):
+        loss_cp(k, plane(k), me_q).start()
+    form(0)
     for j, (h, i) in enumerate(order):
-        pre_send[j] = bank_term(h, 2 * pair_at(i) + 1 - side).astype(BF16)
-        pre_cp(j).start()
-    ug_recv[zc] = user_term(zc)
-    for j, (h, i) in enumerate(order):
+        if j < npair:
+            give(npair + j)
         term = bank_term(h, 2 * pair_at(i) + side)
         pre_cp(j).wait_recv()
         term = (term + pre_recv[j].astype(F32)).astype(BF16)
@@ -291,17 +308,7 @@
             bg_cp(j, goal, me_r).start()
         else:
             bg_recv[me_r] = term
-
-    for k in range(1, nz):
-        z = col(nz - k)
-        posl_cp(k, z, z).wait_recv()
-    pos = posl[0, 0:nz, :]
-    for z in range(1, nz):
-        pos = pos + posl[z, 0:nz, :]
-    part = jnp.sum(wt[...] * (lse - pos), axis=0, keepdims=True)
-    loss_buf[me_q] = jnp.broadcast_to(part, (8, per_dev))
-    for k in range(1, nq):
-        loss_cp(k, plane(k), me_q).start()
+    ug_recv[zc] = user_term(zc)
 
     for k in range(1, nz):
         z = col(nz - k)

time: 28.4 us -> 26.9 us (0.947)
  Pallas kernels: 27.6 us -> 26.1 us
    pallas_call x1, Pallas kernels: 26.3 us -> 24.9 us  [per_device(): pl.pallas_call(functools.partial(kernel, nz, ng), out_shape=(pltpu.VMEM((...]
where the time goes in v4:
time: 26.9 us; the launch traced here: 26.8 us
  Pallas kernels  26.1 us (97%)
  between operations  0.64 us (2%)
    pallas_call x1, Pallas kernels, per_device(): pl.pallas_call(functools.partial(kernel, nz, ng), out_shape=(pltpu.VMEM((...  24.9 us
    pallas_call x1, Pallas kernels, per_device(): pl.pallas_call(functools.partial(finish, per_dev * nz * nq), out_shape=(j...  1.27 us

profile of v4, /device:TPU:0, one launch (start us, length us, event | category | flops | bytes accessed | tf_op | source)
XLA Modules:
  0.0 26.8 jit_solution(10139996283136439107)
XLA Ops:
  0.6 24.9 %shard_map.67 = (f32[8,8,128]{2,1,0:T(8,128)S(1)}, bf16[4,128,256]{2,1,0:T(8,128)(2,1)S(1)}, bf16[4,128,256]{2,1,0:T(8,128)(2,1)S(1)}) custom-call(bf16[128,256]{1,0:T(8,128)(2,1)} %users_hbm.1, bf16[512,256]{1,0:T(8,128)(2,1)} %bank_hbm.1, s32[1,128]{1,0:T(1,128)} %bitcast.3, s32[1,128]{1,0:T(1,128)} %bitcast.4), custom_call_target="tpu_custom_call" | custom-call | tf_op jit(solution)/shard_map/pallas_call | solution.py:368
  25.5 1.3 %shard_map.68 = (f32[1,1]{1,0:T(1,128)}, f32[128,256]{1,0:T(8,128)}, f32[128,256]{1,0:T(8,128)}) custom-call(f32[8,8,128]{2,1,0:T(8,128)S(1)} %get-tuple-element.9.loss_buf, bf16[4,128,256]{2,1,0:T(8,128)(2,1)S(1)} %get-tuple-element.10.ug_recv, bf16[4,128,256]{2,1,0:T(8,128)(2,1)S(1)} %get-tuple-element.11.bg_recv), custom_call_target="tpu_custom_call" | custom-call | tf_op jit(solution)/shard_map/pallas_call | solution.py:410

commit v5 on v4

--- a/solution.py
+++ b/solution.py
@@ -15,10 +15,10 @@
 
 def kernel(
     nz, ng, users_hbm, bank_hbm, pos_hbm, coh_hbm,
-    loss_buf, ug_recv, bg_recv,
+    loss_buf, ug_sum, bg_recv,
     allu, bank_ref, pbank, pos_ref, coh_ref, local, meta_own, meta, ex, dl,
     loc_max, loc_sum, loc_pos, stat, posl, cw, wt,
-    hist, et, ht, ug_send, bg_send, pre_send, pre_recv,
+    hist, et, ht, ug_recv, ug_send, bg_send, pre_send, pre_recv,
     bank_sem, us, ur, ms, mr, ss, sr, ps, pr, gs, gr, hs, hr, ls, lr, bs, br, xs, xr,
 ):
     per_dev = users_hbm.shape[0]
@@ -313,6 +313,10 @@
     for k in range(1, nz):
         z = col(nz - k)
         ug_cp(k, z, z).wait_recv()
+    acc = ug_recv[0].astype(F32)
+    for z in range(1, nz):
+        acc = acc + ug_recv[z].astype(F32)
+    ug_sum[...] = acc
     for k in range(1, nr):
         r = lax.rem(me_r + k, nr)
         bg_cp(k, r, r).wait_recv()
@@ -336,15 +340,17 @@
             bg_cp(j, lax.rem(me_r + 1, nr), me_r).wait_send()
 
 
-def finish(users, loss_buf, ug_recv, bg_recv, loss_ref, ug_hbm, bg_hbm, ug, bg, sem):
-    copies = []
-    for i, (terms, total, out) in enumerate(((ug_recv, ug, ug_hbm), (bg_recv, bg, bg_hbm))):
-        acc = terms[0].astype(F32)
-        for t in range(1, terms.shape[0]):
-            acc = acc + terms[t].astype(F32)
-        total[...] = acc
-        copies.append(pltpu.make_async_copy(total, out, sem.at[i]))
-        copies[-1].start()
+def finish(users, loss_buf, ug, bg_recv, loss_ref, ug_hbm, bg_hbm, bg, sem):
+    copies = [
+        pltpu.make_async_copy(ug, ug_hbm, sem.at[0]),
+        pltpu.make_async_copy(bg, bg_hbm, sem.at[1]),
+    ]
+    copies[0].start()
+    acc = bg_recv[0].astype(F32)
+    for t in range(1, bg_recv.shape[0]):
+        acc = acc + bg_recv[t].astype(F32)
+    bg[...] = acc
+    copies[1].start()
     acc = loss_buf[0, 0:1, :]
     for q in range(1, loss_buf.shape[0]):
         acc = acc + loss_buf[q, 0:1, :]
@@ -369,7 +375,7 @@
             functools.partial(kernel, nz, ng),
             out_shape=(
                 pltpu.VMEM((nq, 8, per_dev), F32),
-                pltpu.VMEM((nz, per_dev, width), BF16),
+                pltpu.VMEM((per_dev, width), F32),
                 pltpu.VMEM((ng, share, width), BF16),
             ),
             in_specs=[anywhere] * 4,
@@ -396,6 +402,7 @@
                 pltpu.VMEM((2, nz, per_dev, width), F32),
                 pltpu.VMEM((nz, per_dev, width), F32),
                 pltpu.VMEM((nz, per_dev, width), BF16),
+                pltpu.VMEM((nz, per_dev, width), BF16),
                 pltpu.VMEM((ng, share, width), BF16),
                 pltpu.VMEM((ng, share, width), BF16),
                 pltpu.VMEM((ng, share, width), BF16),
@@ -417,7 +424,6 @@
             in_specs=[vmem] * 3,
             out_specs=(vmem, anywhere, anywhere),
             scratch_shapes=[
-                pltpu.VMEM((per_dev, width), F32),
                 pltpu.VMEM((share, width), F32),
                 dma((2,)),
             ],

time: 26.9 us -> 26.9 us (level)
  no operation moved by 1% of the time
where the time goes in v5:
time: 26.9 us; the launch traced here: 26.7 us
  Pallas kernels  26.1 us (97%)
  between operations  0.64 us (2%)
    pallas_call x1, Pallas kernels, per_device(): pl.pallas_call(functools.partial(kernel, nz, ng), out_shape=(pltpu.VMEM((...  24.9 us
    pallas_call x1, Pallas kernels, per_device(): pl.pallas_call(functools.partial(finish, per_dev * nz * nq), out_shape=(j...  1.23 us

profile of v5, /device:TPU:0, one launch (start us, length us, event | category | flops | bytes accessed | tf_op | source)
XLA Modules:
  0.0 26.7 jit_solution(15590362874740246779)
XLA Ops:
  0.6 24.9 %shard_map.67 = (f32[8,8,128]{2,1,0:T(8,128)S(1)}, f32[128,256]{1,0:T(8,128)S(1)}, bf16[4,128,256]{2,1,0:T(8,128)(2,1)S(1)}) custom-call(bf16[128,256]{1,0:T(8,128)(2,1)} %users_hbm.1, bf16[512,256]{1,0:T(8,128)(2,1)} %bank_hbm.1, s32[1,128]{1,0:T(1,128)} %bitcast.3, s32[1,128]{1,0:T(1,128)} %bitcast.4), custom_call_target="tpu_custom_call" | custom-call | tf_op jit(solution)/shard_map/pallas_call | solution.py:374
  25.5 1.2 %shard_map.68 = (f32[1,1]{1,0:T(1,128)}, f32[128,256]{1,0:T(8,128)}, f32[128,256]{1,0:T(8,128)}) custom-call(f32[8,8,128]{2,1,0:T(8,128)S(1)} %get-tuple-element.9.loss_buf, f32[128,256]{1,0:T(8,128)S(1)} %get-tuple-element.10.ug, bf16[4,128,256]{2,1,0:T(8,128)(2,1)S(1)} %get-tuple-element.11.bg_recv), custom_call_target="tpu_custom_call" | custom-call | tf_op jit(solution)/shard_map/pallas_call | solution.py:417
